TPU v7x, 32 devices: a whole 2x2x4 slice. The times are simulated.
32 devices in a mesh: fsdp: 8 (over z, x), pipe: 2 (over core), dp: 2 (over y).
Axes of the slice: x: 2, y: 2, z: 4, core: 2. Of those that a mesh axis runs over, the one named last changes fastest.
Arguments:
- video_tokens: bfloat16 [2, 1024, 2560], P('dp', 'fsdp'), may hold values from -6 to 6
- cached_out: bfloat16 [2, 2, 1024, 2560], P('pipe', 'dp', 'fsdp'), may hold values from -6 to 6
- fresh_mask: int32 [2, 2, 1024], P('pipe', 'dp', 'fsdp'), may hold values from 0 to 1, as said below
- timestep: int32 [2], P('dp'), may hold values from 0 to 49
- up_weight: bfloat16 [2, 7168, 2560], P('pipe', 'fsdp'), may hold values from -0.125 to 0.125
- down_weight: bfloat16 [2, 7168, 2560], P('pipe', 'fsdp'), may hold values from -0.0625 to 0.0625
- router_in: bfloat16 [2, 2560, 256], P('pipe', 'fsdp'), may hold values from -0.125 to 0.125
- router_bias: float32 [2, 50, 256], P('pipe'), may hold values from -6 to 6
- router_out: float32 [2, 256], P('pipe'), may hold values from -0.375 to 0.375
- out_cotangent: bfloat16 [2, 1024, 2560], P('dp', 'fsdp'), may hold values from -0.119628906 to 0.119628906
Outputs:
- blended: bfloat16 [2, 2, 1024, 2560], P('pipe', 'dp', 'fsdp')
- grad_router_in: float32 [2, 2560, 256], P('pipe', 'fsdp')
- grad_router_bias: float32 [2, 50, 256], P('pipe')
- grad_router_out: float32 [2, 256], P('pipe')
Inputs may be any that keep to these rules, and one draw needn't show every extreme that they name: `fresh_mask`: for each section and video, the 128 consecutive tokens of one index of fsdp hold 1 to 2 ones, and some index holds exactly 2.
All inputs are finite; a program needn't handle non-finite values.
Results may differ from a plain program's by a relative error of at most 0.023.
Values may be sent and summed in bfloat16 or wider, within the bound.
A program may use at most 64 MiB of HBM per device.

v0:
```python
import jax
import jax.numpy as jnp
from jax import lax
from jax.sharding import PartitionSpec as P

FRESH = 2
layer_eps = 1e-06
gelu_scale = 0.7978845608028654
gelu_cubic = 0.044715


def from_behind(block, axis, distance):
    devices = range(lax.axis_size(axis))
    route = [(i - distance, i) for i in devices if i - distance in devices]
    return lax.ppermute(block, axis, route)


def for_sending(value):
    return jax.tree.map(lambda a: a.astype(jnp.bfloat16) if a.dtype == jnp.float32 else a, value)


def gelu_tanh(values):
    inner_arg = gelu_scale * (values + gelu_cubic * values * values * values)
    return 0.5 * values * (1.0 + jnp.tanh(inner_arg))


def gelu_slope(values):
    inner_arg = gelu_scale * (values + gelu_cubic * values * values * values)
    tanh_val = jnp.tanh(inner_arg)
    return 0.5 * (1.0 + tanh_val) + 0.5 * values * (1.0 - tanh_val * tanh_val) * gelu_scale * (
        1.0 + 3.0 * gelu_cubic * values * values
    )


def normalize(inputs):
    values = inputs.astype(jnp.float32)
    center = values - jnp.mean(values, axis=1, keepdims=True)
    inv_std = lax.rsqrt(jnp.mean(center * center, axis=1, keepdims=True) + layer_eps)
    return (center * inv_std, inv_std)


def normalize_back(scaled, inv_std, grads):
    return inv_std * (
        grads
        - jnp.mean(grads, axis=1, keepdims=True)
        - scaled * jnp.mean(grads * scaled, axis=1, keepdims=True)
    )


def contract_last(left, right):
    return lax.dot_general(
        left, right, (((1,), (1,)), ((), ())), preferred_element_type=jnp.float32
    )


def contract_first(left, right):
    return lax.dot_general(
        left, right, (((0,), (0,)), ((), ())), preferred_element_type=jnp.float32
    )


def gather_gate(gate_grad):
    return lax.all_gather(gate_grad, "fsdp", axis=0, tiled=True)


def body(
    video_tokens,
    cached_out,
    fresh_mask,
    timestep,
    up_weight,
    down_weight,
    router_in,
    router_bias,
    router_out,
    out_cotangent,
):
    section_id = lax.axis_index("pipe")
    column_slot = lax.axis_index("fsdp")
    inputs_first = video_tokens[0]
    cached = cached_out[0, 0]
    mask_row = fresh_mask[0, 0]
    w_up = up_weight[0]
    w_down = down_weight[0]
    r_in = router_in[0]
    r_out = router_out[0]
    tok_rows = inputs_first.shape[0]
    shard_cols = r_in.shape[0]
    hot_step = (jnp.arange(router_bias.shape[1]) == timestep[0]).astype(jnp.float32)
    bias_row = jnp.dot(hot_step, router_bias[0], precision=lax.Precision.HIGHEST)
    picked = jnp.argsort(1 - mask_row, stable=True)[:FRESH]
    live_rows = (jnp.arange(FRESH) < jnp.sum(mask_row)).astype(jnp.float32)

    def select(values):
        return jnp.take(values, picked, axis=0)

    def spread(values):
        return jnp.zeros((tok_rows, values.shape[1]), values.dtype).at[picked].add(values)

    def forward(inputs):
        rows_in = select(inputs)
        rows_cached = select(cached).astype(jnp.float32)
        scaled, inv_std = normalize(rows_in)
        normed = scaled.astype(jnp.bfloat16)
        row_count = normed.shape[0]
        gathered = lax.all_gather(normed, "fsdp", axis=0, tiled=True)
        pre_act = contract_last(gathered, w_up)
        hid_act = gelu_tanh(pre_act).astype(jnp.bfloat16)
        block_sum = lax.psum_scatter(
            jnp.dot(hid_act, w_down, preferred_element_type=jnp.float32).astype(jnp.bfloat16),
            "fsdp",
            scatter_dimension=0,
            tiled=True,
        ).astype(jnp.float32)
        columns = lax.dynamic_slice_in_dim(gathered, column_slot * shard_cols, shard_cols, 1)
        router_part = jnp.dot(columns, r_in, preferred_element_type=jnp.float32)
        router_pre = (
            lax.psum(router_part.astype(jnp.bfloat16), "fsdp").astype(jnp.float32)
            + bias_row[None, :]
        )
        gate_all = jax.nn.sigmoid(
            jnp.dot(gelu_tanh(router_pre), r_out, precision=lax.Precision.HIGHEST)
        )
        gate_own = lax.dynamic_slice_in_dim(gate_all, column_slot * row_count, row_count, 0)
        fresh_out = rows_in.astype(jnp.float32) + block_sum
        delta_rows = live_rows[:, None] * gate_own[:, None] * (fresh_out - rows_cached)
        blended = (cached.astype(jnp.float32) + spread(delta_rows)).astype(jnp.bfloat16)
        stored = (
            scaled,
            inv_std,
            columns,
            pre_act,
            router_pre,
            gate_all,
            gate_own,
            fresh_out,
            rows_cached,
        )
        return (blended, stored)

    def local_grads(stored, cot_rows):
        gate_own = stored[6]
        fresh_out = stored[7]
        rows_cached = stored[8]
        gate_grad = jnp.sum(cot_rows * live_rows[:, None] * (fresh_out - rows_cached), axis=1)
        fresh_grad = cot_rows * (live_rows * gate_own)[:, None]
        return (gate_grad, fresh_grad)

    def router_grads(stored, gate_all_grad):
        columns = stored[2]
        router_pre = stored[4]
        gate_all = stored[5]
        logit_grad = gate_all_grad * gate_all * (1.0 - gate_all)
        out_grad = jnp.dot(logit_grad, gelu_tanh(router_pre), precision=lax.Precision.HIGHEST)
        hidden_grad = logit_grad[:, None] * r_out[None, :] * gelu_slope(router_pre)
        hidden_b = hidden_grad.astype(jnp.bfloat16)
        in_grad = contract_first(columns, hidden_b)
        bias_grad = hot_step[:, None] * jnp.sum(hidden_grad, axis=0)[None, :]
        return (hidden_b, (in_grad, bias_grad, out_grad))

    blended_first, stored_first = forward(inputs_first)
    arriving = from_behind(blended_first, "pipe", 1)
    inputs_second = jnp.where(section_id == 1, arriving, inputs_first)
    blended_out, stored = forward(inputs_second)
    cot_second = select(out_cotangent[0]).astype(jnp.float32)
    gate_grad, fresh_grad = local_grads(stored, cot_second)
    hidden_b, grads_second = router_grads(stored, gather_gate(gate_grad))
    fresh_rows = lax.all_gather(fresh_grad.astype(jnp.bfloat16), "fsdp", axis=0, tiled=True)
    act_grad = contract_last(fresh_rows, w_down)
    pre_grad = (act_grad * gelu_slope(stored[3])).astype(jnp.bfloat16)
    row_count = fresh_grad.shape[0]
    total_rows = jnp.dot(pre_grad, w_up, preferred_element_type=jnp.float32)
    router_term = contract_last(hidden_b, r_in)
    current = lax.dynamic_slice_in_dim(total_rows, column_slot * shard_cols, shard_cols, 1)
    normed_grad = lax.psum_scatter(
        lax.dynamic_update_slice_in_dim(
            total_rows, current + router_term, column_slot * shard_cols, 1
        ).astype(jnp.bfloat16),
        "fsdp",
        scatter_dimension=0,
        tiled=True,
    ).astype(jnp.float32)
    input_grad = fresh_grad + normalize_back(stored[0], stored[1], normed_grad)
    positions = picked.astype(jnp.float32)
    got_rows, got_positions = from_behind((input_grad, positions), "pipe", -1)
    returning = (
        jnp.zeros((tok_rows, input_grad.shape[1]), jnp.float32)
        .at[got_positions.astype(jnp.int32)]
        .add(got_rows)
    )
    gate_grad_first, unused_grad = local_grads(stored, select(returning))
    unused_hidden, grads_first = router_grads(stored, gather_gate(gate_grad_first))
    chosen = tuple(
        (
            jnp.where(section_id == 1, second_grad, first_grad)
            for second_grad, first_grad in zip(grads_second, grads_first)
        )
    )
    summed = jax.tree.map(
        lambda part: part.astype(jnp.float32), lax.psum(for_sending(chosen), "dp")
    )
    return (blended_out[None, None], summed[0][None], summed[1][None], summed[2][None])


def solution(mesh):
    placed = (
        P("dp", "fsdp", None),
        P("pipe", "dp", "fsdp", None),
        P("pipe", "dp", "fsdp"),
        P("dp"),
        P("pipe", "fsdp", None),
        P("pipe", "fsdp", None),
        P("pipe", "fsdp", None),
        P("pipe", None, None),
        P("pipe", None),
        P("dp", "fsdp", None),
    )
    return jax.shard_map(
        body,
        mesh=mesh,
        in_specs=placed,
        out_specs=(
            P("pipe", "dp", "fsdp", None),
            P("pipe", "fsdp", None),
            P("pipe", None, None),
            P("pipe", None),
        ),
        check_vma=False,
    )
```

profile of v0, /device:TPU:0, one launch (start us, length us, event | category | flops | bytes accessed | tf_op | source)
XLA Modules:
  0.0 421.7 jit_solution(18369744704275985153)
XLA Ops:
  7.2 1.3 fusion.193
  8.6 2.5 sort.17
  11.1 1.8 gather_fusion.1
  13.4 32.4 %all-gather = bf16[8,2,2560]{2,1,0:T(2,128)(2,1)S(1)} all-gather(bf16[1,2,2560]{2,1,0:T(2,128)(2,1)S(1)} %fusion.127), channel_id=1, replica_groups=mesh['fsdp'=8,'pipe'=2,'dp'=2] {'fsdp'}, dimensions={0}, use_global_device_ids=true | all-gather | bytes 92160 | tf_op jit(solution)/shard_map/all_gather | solution.py:106
  45.8 6.5 %fusion.12 = bf16[16,2560]{1,0:T(8,128)(2,1)} fusion(bf16[1,896,2560]{2,1,0:T(8,128)(2,1)} %param.17, bf16[16,2560]{1,0:T(8,128)(2,1)S(1)} %reshape.151, bf16[1,896,2560]{2,1,0:T(8,128)(2,1)} %param.16), kind=kOutput, calls=%fused_computation.20 | convolution fusion | flops 146970624 | bytes 9338880 | tf_op jit(solution)/shard_map/dot_general | solution.py:110
  52.7 21.6 %psum.35 = bf16[16,256]{1,0:T(8,128)(2,1)S(1)} all-reduce(bf16[16,256]{1,0:T(8,128)(2,1)S(1)} %convolution_convert_fusion.1), channel_id=1, replica_groups=mesh['fsdp'=8,'pipe'=2,'dp'=2] {'fsdp'}, use_global_device_ids=true, to_apply=%region_4.6 | all-reduce | flops 4096 | bytes 16384 | tf_op jit(solution)/shard_map/psum | solution.py:118
  75.0 0.6 gather_fusion.2
  75.9 0.6 fusion.192
  77.3 0.7 dynamic-slice_select_fusion.1
  78.0 45.0 %all-reduce.13.cloned.1.call-done = bf16[16,2560]{1,0:T(8,128)(2,1)} async-done(((bf16[16,2560]{1,0:T(8,128)(2,1)}), bf16[16,2560]{1,0:T(8,128)(2,1)}) %all-reduce.13.cloned.1.call-update) | async-done | bytes 81936
  123.0 1.4 scatter_custom_fusion
  124.4 0.9 convert_element_type.120
  125.3 1.3 collective-permute-start
  126.7 1.3 collective-permute-start.1
  128.0 0.6 gather_fusion.4
  129.1 0.7 fusion.156
  129.8 1.2 broadcast_select_fusion
  131.0 0.6 gather_fusion.3
  132.1 30.5 %all-gather.1 = bf16[8,2,2560]{2,1,0:T(2,128)(2,1)S(1)} all-gather(bf16[1,2,2560]{2,1,0:T(2,128)(2,1)S(1)} %fusion.126), channel_id=1, replica_groups=mesh['fsdp'=8,'pipe'=2,'dp'=2] {'fsdp'}, dimensions={0}, use_global_device_ids=true | all-gather | bytes 92160 | tf_op jit(solution)/shard_map/all_gather | solution.py:106
  162.7 3.6 fusion.8
  166.5 3.7 fusion.15
  170.2 20.5 %psum.36 = bf16[16,256]{1,0:T(8,128)(2,1)S(1)} all-reduce(bf16[16,256]{1,0:T(8,128)(2,1)S(1)} %convolution_convert_fusion), channel_id=1, replica_groups=mesh['fsdp'=8,'pipe'=2,'dp'=2] {'fsdp'}, use_global_device_ids=true, to_apply=%region_9.11 | all-reduce | flops 4096 | bytes 16384 | tf_op jit(solution)/shard_map/psum | solution.py:118
  190.8 0.7 dynamic-slice_select_fusion
  191.6 48.1 %all-reduce.15.cloned.1.call-done = bf16[16,2560]{1,0:T(8,128)(2,1)} async-done(((bf16[16,2560]{1,0:T(8,128)(2,1)}), bf16[16,2560]{1,0:T(8,128)(2,1)}) %all-reduce.15.cloned.1.call-update) | async-done | bytes 81936
  239.6 1.0 fusion.93
  240.6 30.5 %all-gather.2 = bf16[8,2,2560]{2,1,0:T(2,128)(2,1)S(1)} all-gather(bf16[1,2,2560]{2,1,0:T(2,128)(2,1)S(1)} %get-tuple-element.21), channel_id=1, replica_groups=mesh['fsdp'=8,'pipe'=2,'dp'=2] {'fsdp'}, dimensions={0}, use_global_device_ids=true | all-gather | bytes 92160 | tf_op jit(solution)/shard_map/all_gather | solution.py:168
  271.2 0.2 dynamic-update-slice
  271.5 5.8 %fusion.6 = f32[16,2560]{1,0:T(8,128)S(1)} fusion(bf16[1,896,2560]{2,1,0:T(8,128)(2,1)} %param.16, bf16[16,2560]{1,0:T(8,128)(2,1)S(1)} %reshape.155, bf16[1,896,2560]{2,1,0:T(8,128)(2,1)} %param.17, f32[16,896]{1,0:T(8,128)S(1)} %fusion.8), kind=kOutput, calls=%fused_computation.14 | convolution fusion | flops 147073024 | bytes 9478144 | tf_op jit(solution)/shard_map/dot_general | solution.py:172
  277.3 20.1 %all-reduce = f32[16]{0:T(128)S(1)} all-reduce(f32[16]{0:T(128)S(1)} %dynamic-update-slice), channel_id=1, replica_groups=mesh['fsdp'=8,'pipe'=2,'dp'=2] {'fsdp'}, use_global_device_ids=true, to_apply=%add | all-reduce | flops 16 | bytes 128
  297.6 0.4 dynamic_update_slice.3
  298.0 0.6 convert_element_type.136
  298.7 1.2 scatter_custom_fusion.1
  299.9 0.9 convert_bitcast_fusion
  300.8 64.7 %all-reduce.17.cloned.1.call-done = bf16[16,2560]{1,0:T(8,128)(2,1)} async-done(((bf16[16,2560]{1,0:T(8,128)(2,1)}), bf16[16,2560]{1,0:T(8,128)(2,1)}) %all-reduce.17.cloned.1.call-update) | async-done | bytes 81936
  365.6 1.0 convert_reduce_fusion
  366.6 0.9 fusion.80
  367.5 1.3 collective-permute-start.2
  368.8 0.3 fusion.129
  369.1 1.5 collective-permute-done.2
  370.5 1.0 scatter_custom_fusion.2
  371.5 0.6 gather_fusion
  372.7 20.2 %all-reduce.1 = f32[16]{0:T(128)S(1)} all-reduce(f32[16]{0:T(128)S(1)} %dynamic-update-slice.1), channel_id=1, replica_groups=mesh['fsdp'=8,'pipe'=2,'dp'=2] {'fsdp'}, use_global_device_ids=true, to_apply=%add.1 | all-reduce | flops 16 | bytes 128
  393.1 1.0 fusion.19
  394.2 8.9 %all-reduce.5 = (bf16[1,50,256]{2,0,1:T(2,128)(2,1)S(1)}, bf16[1,256]{1,0:T(2,128)(2,1)S(1)}) all-reduce(bf16[1,50,256]{2,0,1:T(2,128)(2,1)S(1)} %broadcast_in_dim.75, bf16[1,256]{1,0:T(2,128)(2,1)S(1)} %broadcast_in_dim.77), channel_id=1, replica_groups=mesh['fsdp'=8,'pipe'=2,'dp'=2] {'dp'}, use_global_device_ids=true, to_apply=%region_21.23 | all-reduce | flops 13056 | bytes 52224 | tf_op jit(solution)/shard_map/psum | solution.py:200
  403.1 0.7 broadcast_in_dim.76
  403.8 0.6 broadcast_in_dim.78
  404.4 9.1 %all-reduce.11.cloned.1.call-done = bf16[1,320,256]{2,1,0:T(8,128)(2,1)} async-done(((bf16[1,320,256]{2,1,0:T(8,128)(2,1)}), bf16[1,320,256]{2,1,0:T(8,128)(2,1)}) %all-reduce.11.cloned.1.call-update) | async-done | bytes 163856 | tf_op jit(solution)/shard_map/psum | solution.py:200
  413.5 1.7 broadcast_in_dim.74
  (63 shorter events, 3.6 us)
Async XLA Ops:
  7.2 120.8 %copy-start = (bf16[1,128,2560]{2,1,0:T(8,128)(2,1)S(1)}, bf16[1,128,2560]{2,1,0:T(8,128)(2,1)}, u32[]{:S(2)}) copy-start(bf16[1,128,2560]{2,1,0:T(8,128)(2,1)} %param.21) | copy-start | bytes 1966084
  7.2 115.8 %all-reduce.13.cloned.1.call-start = ((), (), s32[]{:S(2)}) async-start(), calls=%async_computation.1 | async-start | bytes 163840
  45.8 6.6 %copy-start.1 = (bf16[1,320,256]{2,1,0:T(8,128)(2,1)S(1)}, bf16[1,320,256]{2,1,0:T(8,128)(2,1)}, u32[]{:S(2)}) copy-start(bf16[1,320,256]{2,1,0:T(8,128)(2,1)} %param.18) | copy-start | bytes 491524
  45.8 29.1 %copy-start.2 = (bf16[1,1,128,2560]{3,2,1,0:T(8,128)(2,1)S(1)}, bf16[1,1,128,2560]{3,2,1,0:T(8,128)(2,1)}, u32[]{:S(2)}) copy-start(bf16[1,1,128,2560]{3,2,1,0:T(8,128)(2,1)} %param.13) | copy-start | bytes 1966084
  52.3 23.4 %copy-start.3 = (f32[1,50,256]{2,0,1:T(1,128)S(1)}, f32[1,50,256]{2,0,1:T(1,128)}, u32[]{:S(2)}) copy-start(f32[1,50,256]{2,0,1:T(1,128)} %param.19) | copy-start | bytes 153604
  52.4 23.5 %copy-start.5 = (u32[32]{0:T(128)S(1)}, u32[32]{0:T(128)}, u32[]{:S(2)}) copy-start(u32[32]{0:T(128)} %constant.94) | copy-start | bytes 388
  52.4 24.8 %copy-start.4 = (f32[1,256]{1,0:T(1,128)S(1)}, f32[1,256]{1,0:T(1,128)}, u32[]{:S(2)}) copy-start(f32[1,256]{1,0:T(1,128)} %param.20) | copy-start | bytes 3076
  52.4 187.3 %all-reduce.15.cloned.1.call-start = ((), (), s32[]{:S(2)}) async-start(), calls=%async_computation.2 | async-start | bytes 163840
  125.3 4.5 %collective-permute-start = (bf16[128,2560]{1,0:T(8,128)(2,1)}, bf16[128,2560]{1,0:T(8,128)(2,1)S(1)}, u32[]{:S(2)}, u32[]{:S(2)}) collective-permute-start(bf16[128,2560]{1,0:T(8,128)(2,1)} %convert_element_type.120), channel_id=1, source_target_pairs={{0,2},{1,3},{4,6},{5,7},{8,10},{9,11},{12,14},{13,15},{16,18},{17,... | collective-permute-start | bytes 1966088 | tf_op jit(solution)/shard_map/ppermute | solution.py:15
  126.7 3.1 collective-permute-start.1
  170.2 195.4 %all-reduce.17.cloned.1.call-start = ((), (), s32[]{:S(2)}) async-start(), calls=%async_computation.3 | async-start | bytes 163840
  298.6 114.8 %all-reduce.11.cloned.1.call-start = ((), (), s32[]{:S(2)}) async-start(), calls=%async_computation | async-start | bytes 327680 | tf_op jit(solution)/shard_map/psum | solution.py:200
  367.5 3.1 collective-permute-start.2
Sparse Core Ops, SparseCore 0:
  52.5 70.4 all-reduce.12
  170.3 69.3 all-reduce.14
  298.8 66.7 all-reduce.16
  394.2 19.2 all-reduce.10
where the time goes:
time: 422 us
  blocking collectives  185 us (44%)
  waiting for transfers between devices  168 us (40%)
  matrix products  22.2 us (5%)
  other arithmetic  20.6 us (5%)
  between operations  16 us (4%)
  local copies, waits for them, and re-layouts  5.75 us (1%)
    unnamed x7, waiting for transfers between devices  158 us
    all_gather x2, blocking collectives, forward(): gathered = lax.all_gather(normed, 'fsdp', axis=0, tiled=True)  62.9 us
    psum x2, blocking collectives, forward(): lax.psum(router_part.astype(jnp.bfloat16), 'fsdp').astype(jnp.float32)  42.1 us
    unnamed x2, blocking collectives  40.3 us
    all_gather x1, blocking collectives, body(): lax.all_gather(fresh_grad.astype(jnp.bfloat16), 'fsdp', axis=0, tiled=True)  30.5 us
    dot_general x2, matrix products, forward(): jnp.dot(hid_act, w_down, preferred_element_type=jnp.float32)  10.2 us
    psum x1, waiting for transfers between devices, body(): lax.psum(for_sending(chosen), 'dp')  9.1 us
    psum x1, blocking collectives, body(): lax.psum(for_sending(chosen), 'dp')  8.92 us
  transfers between devices with their start and end apart: 7, of which 5 were waited for; matrix products, arithmetic and copies ran while one was open for 2% of the time, Pallas kernels for 0%

commit v1 on v0

--- a/solution.py
+++ b/solution.py
@@ -7,6 +7,19 @@
 layer_eps = 1e-06
 gelu_scale = 0.7978845608028654
 gelu_cubic = 0.044715
+
+
+def fix_limits_here(u):
+    dev_n = lax.axis_size("fsdp")
+    piece_next = list(map(lambda j: (j - 1, j), range(1, dev_n)))
+    y2 = u
+    answer = piece_next + [(dev_n - 1, 0)]
+    line_up = [y2]
+    for _ in [*range(dev_n - 1)]:
+        y2 = lax.ppermute(y2, "fsdp", answer)
+        line_up += [y2]
+    raw_out = jnp.concatenate([*reversed(line_up)], axis=0)
+    return jnp.roll(raw_out, (lax.axis_index("fsdp") + 1) * y2.shape[0], axis=0)
 
 
 def from_behind(block, axis, distance):
@@ -103,7 +116,7 @@
         scaled, inv_std = normalize(rows_in)
         normed = scaled.astype(jnp.bfloat16)
         row_count = normed.shape[0]
-        gathered = lax.all_gather(normed, "fsdp", axis=0, tiled=True)
+        gathered = fix_limits_here(normed)
         pre_act = contract_last(gathered, w_up)
         hid_act = gelu_tanh(pre_act).astype(jnp.bfloat16)
         block_sum = lax.psum_scatter(

time: 422 us -> 467 us (1.11)
  waiting for transfers between devices: 168 us -> 268 us
  blocking collectives: 185 us -> 118 us
    ppermute x0 -> x14, waiting for transfers between devices: none -> 75.8 us  [fix_limits_here(): y2 = lax.ppermute(y2, 'fsdp', answer)]
    all_gather x2 -> x0, blocking collectives: 62.9 us -> none  [forward(): gathered = lax.all_gather(normed, 'fsdp', axis=0, tiled=True)]
    unnamed x7, waiting for transfers between devices: 158 us -> 181 us
  transfers between devices with their start and end apart: 7 -> 21, of which waited for: 5 -> 20; matrix products, arithmetic and copies ran while one was open for 2% -> 6% of each run, Pallas kernels for 0% -> 0%
where the time goes in v1:
time: 467 us; the launch traced here: 466 us
  waiting for transfers between devices  268 us (57%)
  blocking collectives  118 us (25%)
  matrix products  24.4 us (5%)
  other arithmetic  22.8 us (5%)
  between operations  16.1 us (3%)
  starting transfers between devices  8.38 us (2%)
  local copies, waits for them, and re-layouts  8.02 us (2%)
    unnamed x7, waiting for transfers between devices  181 us
    ppermute x14, waiting for transfers between devices, fix_limits_here(): y2 = lax.ppermute(y2, 'fsdp', answer)  75.8 us
    unnamed x2, blocking collectives  40.3 us
    psum x2, blocking collectives, forward(): lax.psum(router_part.astype(jnp.bfloat16), 'fsdp').astype(jnp.float32)  37.9 us
    all_gather x1, blocking collectives, body(): lax.all_gather(fresh_grad.astype(jnp.bfloat16), 'fsdp', axis=0, tiled=True)  30.5 us
    dot_general x2, matrix products, forward(): jnp.dot(hid_act, w_down, preferred_element_type=jnp.float32)  10.2 us
  transfers between devices with their start and end apart: 21, of which 20 were waited for; matrix products, arithmetic and copies ran while one was open for 6% of the time, Pallas kernels for 0%

profile of v1, /device:TPU:0, one launch (start us, length us, event | category | flops | bytes accessed | tf_op | source)
XLA Modules:
  0.0 465.6 jit_solution(680879602119435941)
XLA Ops:
  7.2 1.3 fusion.204
  8.6 2.5 sort.17
  11.6 1.8 gather_fusion.1
  13.9 3.0 collective-permute-start
  16.9 4.7 %collective-permute-done = bf16[2,2560]{1,0:T(2,128)(2,1)S(1)} collective-permute-done((bf16[2,2560]{1,0:T(2,128)(2,1)S(1)}, bf16[2,2560]{1,0:T(2,128)(2,1)S(1)}, u32[]{:S(2)}, u32[]{:S(2)}) %collective-permute-start) | collective-permute-done | bytes 10272 | tf_op jit(solution)/shard_map/ppermute | solution.py:19
  21.6 6.4 %collective-permute-done.1 = bf16[2,2560]{1,0:T(2,128)(2,1)S(1)} collective-permute-done((bf16[2,2560]{1,0:T(2,128)(2,1)S(1)}, bf16[2,2560]{1,0:T(2,128)(2,1)S(1)}, u32[]{:S(2)}, u32[]{:S(2)}) %collective-permute-start.1) | collective-permute-done | bytes 10272 | tf_op jit(solution)/shard_map/ppermute | solution.py:19
  28.0 6.4 %collective-permute-done.2 = bf16[2,2560]{1,0:T(2,128)(2,1)S(1)} collective-permute-done((bf16[2,2560]{1,0:T(2,128)(2,1)S(1)}, bf16[2,2560]{1,0:T(2,128)(2,1)S(1)}, u32[]{:S(2)}, u32[]{:S(2)}) %collective-permute-start.2) | collective-permute-done | bytes 10272 | tf_op jit(solution)/shard_map/ppermute | solution.py:19
  34.4 6.4 %collective-permute-done.3 = bf16[2,2560]{1,0:T(2,128)(2,1)S(1)} collective-permute-done((bf16[2,2560]{1,0:T(2,128)(2,1)S(1)}, bf16[2,2560]{1,0:T(2,128)(2,1)S(1)}, u32[]{:S(2)}, u32[]{:S(2)}) %collective-permute-start.3) | collective-permute-done | bytes 10272 | tf_op jit(solution)/shard_map/ppermute | solution.py:19
  40.7 6.4 %collective-permute-done.4 = bf16[2,2560]{1,0:T(2,128)(2,1)S(1)} collective-permute-done((bf16[2,2560]{1,0:T(2,128)(2,1)S(1)}, bf16[2,2560]{1,0:T(2,128)(2,1)S(1)}, u32[]{:S(2)}, u32[]{:S(2)}) %collective-permute-start.4) | collective-permute-done | bytes 10272 | tf_op jit(solution)/shard_map/ppermute | solution.py:19
  47.1 1.2 bitcast_convert_fusion
  49.0 4.5 collective-permute-done.5
  53.5 1.5 fusion.56
  55.0 1.7 gather_fusion.2
  58.2 1.7 collective-permute-done.6
  60.0 6.5 %fusion.12 = bf16[16,2560]{1,0:T(8,128)(2,1)} fusion(bf16[1,896,2560]{2,1,0:T(8,128)(2,1)} %param.19, bf16[1,896,2560]{2,1,0:T(8,128)(2,1)} %param.18, s32[]{:T(128)S(6)} %select_n.96, bf16[16,2560]{1,0:T(8,128)(2,1)S(1)} %concatenate.9), kind=kOutput, calls=%fused_computation.20 | convolution fusion | flops 147134464 | bytes 9338884 | tf_op jit(solution)/shard_map/dot_general | solution.py:123
  66.8 20.5 %psum.35 = bf16[16,256]{1,0:T(8,128)(2,1)S(1)} all-reduce(bf16[16,256]{1,0:T(8,128)(2,1)S(1)} %convolution_convert_fusion.1), channel_id=1, replica_groups=mesh['fsdp'=8,'pipe'=2,'dp'=2] {'fsdp'}, use_global_device_ids=true, to_apply=%region_4.7 | all-reduce | flops 4096 | bytes 16384 | tf_op jit(solution)/shard_map/psum | solution.py:131
  88.8 47.3 %all-reduce.13.cloned.1.call-done = bf16[16,2560]{1,0:T(8,128)(2,1)} async-done(((bf16[16,2560]{1,0:T(8,128)(2,1)}), bf16[16,2560]{1,0:T(8,128)(2,1)}) %all-reduce.13.cloned.1.call-update) | async-done | bytes 81936
  136.2 1.4 scatter_custom_fusion
  138.5 1.3 collective-permute-start.7
  139.9 1.9 collective-permute-done.7
  141.7 1.2 broadcast_select_fusion
  144.8 1.3 collective-permute-start.8
  146.1 5.1 %collective-permute-done.8 = bf16[2,2560]{1,0:T(2,128)(2,1)S(1)} collective-permute-done((bf16[2,2560]{1,0:T(2,128)(2,1)S(1)}, bf16[2,2560]{1,0:T(2,128)(2,1)S(1)}, u32[]{:S(2)}, u32[]{:S(2)}) %collective-permute-start.8) | collective-permute-done | bytes 10272 | tf_op jit(solution)/shard_map/ppermute | solution.py:19
  151.2 6.4 %collective-permute-done.9 = bf16[2,2560]{1,0:T(2,128)(2,1)S(1)} collective-permute-done((bf16[2,2560]{1,0:T(2,128)(2,1)S(1)}, bf16[2,2560]{1,0:T(2,128)(2,1)S(1)}, u32[]{:S(2)}, u32[]{:S(2)}) %collective-permute-start.9) | collective-permute-done | bytes 10272 | tf_op jit(solution)/shard_map/ppermute | solution.py:19
  157.6 6.4 %collective-permute-done.10 = bf16[2,2560]{1,0:T(2,128)(2,1)S(1)} collective-permute-done((bf16[2,2560]{1,0:T(2,128)(2,1)S(1)}, bf16[2,2560]{1,0:T(2,128)(2,1)S(1)}, u32[]{:S(2)}, u32[]{:S(2)}) %collective-permute-start.10) | collective-permute-done | bytes 10272 | tf_op jit(solution)/shard_map/ppermute | solution.py:19
  164.0 6.4 %collective-permute-done.11 = bf16[2,2560]{1,0:T(2,128)(2,1)S(1)} collective-permute-done((bf16[2,2560]{1,0:T(2,128)(2,1)S(1)}, bf16[2,2560]{1,0:T(2,128)(2,1)S(1)}, u32[]{:S(2)}, u32[]{:S(2)}) %collective-permute-start.11) | collective-permute-done | bytes 10272 | tf_op jit(solution)/shard_map/ppermute | solution.py:19
  170.9 1.3 collective-permute-start.15
  172.2 4.5 collective-permute-done.12
  177.3 5.8 %collective-permute-done.13 = bf16[2,2560]{1,0:T(2,128)(2,1)S(1)} collective-permute-done((bf16[2,2560]{1,0:T(2,128)(2,1)S(1)}, bf16[2,2560]{1,0:T(2,128)(2,1)S(1)}, u32[]{:S(2)}, u32[]{:S(2)}) %collective-permute-start.13) | collective-permute-done | bytes 10272 | tf_op jit(solution)/shard_map/ppermute | solution.py:19
  184.5 5.0 %collective-permute-done.14 = bf16[2,2560]{1,0:T(2,128)(2,1)S(1)} collective-permute-done((bf16[2,2560]{1,0:T(2,128)(2,1)S(1)}, bf16[2,2560]{1,0:T(2,128)(2,1)S(1)}, u32[]{:S(2)}, u32[]{:S(2)}) %collective-permute-start.14) | collective-permute-done | bytes 10272 | tf_op jit(solution)/shard_map/ppermute | solution.py:19
  189.8 3.6 fusion.8
  193.4 17.4 %psum.36 = bf16[16,256]{1,0:T(8,128)(2,1)S(1)} all-reduce(bf16[16,256]{1,0:T(8,128)(2,1)S(1)} %convolution_convert_fusion), channel_id=1, replica_groups=mesh['fsdp'=8,'pipe'=2,'dp'=2] {'fsdp'}, use_global_device_ids=true, to_apply=%region_9.12 | all-reduce | flops 4096 | bytes 16384 | tf_op jit(solution)/shard_map/psum | solution.py:131
  211.0 3.7 fusion.15
  215.4 67.7 %all-reduce.15.cloned.1.call-done = bf16[16,2560]{1,0:T(8,128)(2,1)} async-done(((bf16[16,2560]{1,0:T(8,128)(2,1)}), bf16[16,2560]{1,0:T(8,128)(2,1)}) %all-reduce.15.cloned.1.call-update) | async-done | bytes 81936
  283.1 1.0 fusion.101
  284.3 20.1 %all-reduce = f32[16]{0:T(128)S(1)} all-reduce(f32[16]{0:T(128)S(1)} %dynamic-update-slice), channel_id=1, replica_groups=mesh['fsdp'=8,'pipe'=2,'dp'=2] {'fsdp'}, use_global_device_ids=true, to_apply=%add | all-reduce | flops 16 | bytes 128
  304.5 30.5 %all-gather = bf16[8,2,2560]{2,1,0:T(2,128)(2,1)S(1)} all-gather(bf16[1,2,2560]{2,1,0:T(2,128)(2,1)S(1)} %get-tuple-element.22), channel_id=1, replica_groups=mesh['fsdp'=8,'pipe'=2,'dp'=2] {'fsdp'}, dimensions={0}, use_global_device_ids=true | all-gather | bytes 92160 | tf_op jit(solution)/shard_map/all_gather | solution.py:181
  335.0 5.8 %fusion.6 = f32[16,2560]{1,0:T(8,128)S(1)} fusion(bf16[1,896,2560]{2,1,0:T(8,128)(2,1)} %param.18, bf16[16,2560]{1,0:T(8,128)(2,1)S(1)} %reshape.151, bf16[1,896,2560]{2,1,0:T(8,128)(2,1)} %param.19, f32[16,896]{1,0:T(8,128)S(1)} %fusion.8), kind=kOutput, calls=%fused_computation.14 | convolution fusion | flops 147073024 | bytes 9478144 | tf_op jit(solution)/shard_map/dot_general | solution.py:185
  342.1 1.3 scatter_custom_fusion.1
  343.5 65.5 %all-reduce.17.cloned.1.call-done = bf16[16,2560]{1,0:T(8,128)(2,1)} async-done(((bf16[16,2560]{1,0:T(8,128)(2,1)}), bf16[16,2560]{1,0:T(8,128)(2,1)}) %all-reduce.17.cloned.1.call-update) | async-done | bytes 81936
  409.0 1.0 convert_reduce_fusion
  410.9 1.3 collective-permute-start.16
  414.0 1.0 scatter_custom_fusion.2
  416.2 20.2 %all-reduce.1 = f32[16]{0:T(128)S(1)} all-reduce(f32[16]{0:T(128)S(1)} %dynamic-update-slice.1), channel_id=1, replica_groups=mesh['fsdp'=8,'pipe'=2,'dp'=2] {'fsdp'}, use_global_device_ids=true, to_apply=%add.1 | all-reduce | flops 16 | bytes 128
  437.0 1.0 fusion.19
  438.1 8.9 %all-reduce.5 = (bf16[1,50,256]{2,0,1:T(2,128)(2,1)S(1)}, bf16[1,256]{1,0:T(2,128)(2,1)S(1)}) all-reduce(bf16[1,50,256]{2,0,1:T(2,128)(2,1)S(1)} %broadcast_in_dim.75, bf16[1,256]{1,0:T(2,128)(2,1)S(1)} %broadcast_in_dim.77), channel_id=1, replica_groups=mesh['fsdp'=8,'pipe'=2,'dp'=2] {'dp'}, use_global_device_ids=true, to_apply=%region_21.24 | all-reduce | flops 13056 | bytes 52224 | tf_op jit(solution)/shard_map/psum | solution.py:213
  448.3 9.1 %all-reduce.11.cloned.1.call-done = bf16[1,320,256]{2,1,0:T(8,128)(2,1)} async-done(((bf16[1,320,256]{2,1,0:T(8,128)(2,1)}), bf16[1,320,256]{2,1,0:T(8,128)(2,1)}) %all-reduce.11.cloned.1.call-update) | async-done | bytes 163856 | tf_op jit(solution)/shard_map/psum | solution.py:213
  457.4 1.7 broadcast_in_dim.74
  (97 shorter events, 17.1 us)
Async XLA Ops:
  7.2 175.9 %copy-start = (bf16[1,128,2560]{2,1,0:T(8,128)(2,1)S(1)}, bf16[1,128,2560]{2,1,0:T(8,128)(2,1)}, u32[]{:S(2)}) copy-start(bf16[1,128,2560]{2,1,0:T(8,128)(2,1)} %param.23) | copy-start | bytes 1966084
  7.2 49.7 %copy-start.7 = (u32[32]{0:T(128)S(1)}, u32[32]{0:T(128)}, u32[]{:S(2)}) copy-start(u32[32]{0:T(128)} %constant.111) | copy-start | bytes 388
  7.2 129.0 %all-reduce.13.cloned.1.call-start = ((), (), s32[]{:S(2)}) async-start(), calls=%async_computation.1 | async-start | bytes 163840
  11.1 0.5 copy-start.9
  11.1 45.6 %copy-start.3 = (pred[2]{0:T(512)(128)(4,1)}, pred[2]{0:T(512)(128)(4,1)S(1)}, u32[]{:S(2)}) copy-start(pred[2]{0:T(512)(128)(4,1)S(1)} %get-tuple-element.20) | copy-start | bytes 10
  11.1 48.7 %copy-start.8 = (s32[2]{0:T(128)}, s32[2]{0:T(128)S(1)}, u32[]{:S(2)}) copy-start(s32[2]{0:T(128)S(1)} %get-tuple-element.21) | copy-start | bytes 28
  11.6 46.5 %copy-start.6 = (s32[1024]{0:T(1024)}, s32[1024]{0:T(1024)S(1)}, u32[]{:S(2)}) copy-start(s32[1024]{0:T(1024)S(1)} %pad_clamp_fusion) | copy-start | bytes 12292
  13.9 7.7 %collective-permute-start = (bf16[2,2560]{1,0:T(2,128)(2,1)S(1)}, bf16[2,2560]{1,0:T(2,128)(2,1)S(1)}, u32[]{:S(2)}, u32[]{:S(2)}) collective-permute-start(bf16[2,2560]{1,0:T(2,128)(2,1)S(1)} %fusion.96), channel_id=1, source_target_pairs={{0,4},{4,8},{8,12},{12,16},{16,20},{20,24},{24,28},{28,0},{1,5},{5... | collective-permute-start | bytes 30728 | tf_op jit(solution)/shard_map/ppermute | solution.py:19
  21.6 6.4 %collective-permute-start.1 = (bf16[2,2560]{1,0:T(2,128)(2,1)S(1)}, bf16[2,2560]{1,0:T(2,128)(2,1)S(1)}, u32[]{:S(2)}, u32[]{:S(2)}) collective-permute-start(bf16[2,2560]{1,0:T(2,128)(2,1)S(1)} %collective-permute-done), channel_id=1, source_target_pairs={{0,4},{4,8},{8,12},{12,16},{16,20},{20,24},{24,28},{28,0},{1,5},{5... | collective-permute-start | bytes 30728 | tf_op jit(solution)/shard_map/ppermute | solution.py:19
  28.0 6.4 %collective-permute-start.2 = (bf16[2,2560]{1,0:T(2,128)(2,1)S(1)}, bf16[2,2560]{1,0:T(2,128)(2,1)S(1)}, u32[]{:S(2)}, u32[]{:S(2)}) collective-permute-start(bf16[2,2560]{1,0:T(2,128)(2,1)S(1)} %collective-permute-done.1), channel_id=1, source_target_pairs={{0,4},{4,8},{8,12},{12,16},{16,20},{20,24},{24,28},{28,0},{1,5},{5... | collective-permute-start | bytes 30728 | tf_op jit(solution)/shard_map/ppermute | solution.py:19
  34.4 6.4 %collective-permute-start.3 = (bf16[2,2560]{1,0:T(2,128)(2,1)S(1)}, bf16[2,2560]{1,0:T(2,128)(2,1)S(1)}, u32[]{:S(2)}, u32[]{:S(2)}) collective-permute-start(bf16[2,2560]{1,0:T(2,128)(2,1)S(1)} %collective-permute-done.2), channel_id=1, source_target_pairs={{0,4},{4,8},{8,12},{12,16},{16,20},{20,24},{24,28},{28,0},{1,5},{5... | collective-permute-start | bytes 30728 | tf_op jit(solution)/shard_map/ppermute | solution.py:19
  40.7 6.4 %collective-permute-start.4 = (bf16[2,2560]{1,0:T(2,128)(2,1)S(1)}, bf16[2,2560]{1,0:T(2,128)(2,1)S(1)}, u32[]{:S(2)}, u32[]{:S(2)}) collective-permute-start(bf16[2,2560]{1,0:T(2,128)(2,1)S(1)} %collective-permute-done.3), channel_id=1, source_target_pairs={{0,4},{4,8},{8,12},{12,16},{16,20},{20,24},{24,28},{28,0},{1,5},{5... | collective-permute-start | bytes 30728 | tf_op jit(solution)/shard_map/ppermute | solution.py:19
  47.1 6.4 %collective-permute-start.5 = (bf16[2,2560]{1,0:T(2,128)(2,1)S(1)}, bf16[2,2560]{1,0:T(2,128)(2,1)S(1)}, u32[]{:S(2)}, u32[]{:S(2)}) collective-permute-start(bf16[2,2560]{1,0:T(2,128)(2,1)S(1)} %collective-permute-done.4), channel_id=1, source_target_pairs={{0,4},{4,8},{8,12},{12,16},{16,20},{20,24},{24,28},{28,0},{1,5},{5... | collective-permute-start | bytes 30728 | tf_op jit(solution)/shard_map/ppermute | solution.py:19
  53.5 6.4 %collective-permute-start.6 = (bf16[2,2560]{1,0:T(2,128)(2,1)S(1)}, bf16[2,2560]{1,0:T(2,128)(2,1)S(1)}, u32[]{:S(2)}, u32[]{:S(2)}) collective-permute-start(bf16[2,2560]{1,0:T(2,128)(2,1)S(1)} %collective-permute-done.5), channel_id=1, source_target_pairs={{0,4},{4,8},{8,12},{12,16},{16,20},{20,24},{24,28},{28,0},{1,5},{5... | collective-permute-start | bytes 30728 | tf_op jit(solution)/shard_map/ppermute | solution.py:19
  60.0 6.6 %copy-start.1 = (bf16[1,320,256]{2,1,0:T(8,128)(2,1)S(1)}, bf16[1,320,256]{2,1,0:T(8,128)(2,1)}, u32[]{:S(2)}) copy-start(bf16[1,320,256]{2,1,0:T(8,128)(2,1)} %param.20) | copy-start | bytes 491524
  66.5 216.6 %all-reduce.15.cloned.1.call-start = ((), (), s32[]{:S(2)}) async-start(), calls=%async_computation.2 | async-start | bytes 163840
  137.6 73.2 %copy-start.2 = (f32[1,256]{1,0:T(1,128)S(1)}, f32[1,256]{1,0:T(1,128)}, u32[]{:S(2)}) copy-start(f32[1,256]{1,0:T(1,128)} %fusion.56) | copy-start | bytes 3076
  137.6 73.2 %copy-start.5 = (f32[1,256]{1,0:T(1,128)S(1)}, f32[1,256]{1,0:T(1,128)}, u32[]{:S(2)}) copy-start(f32[1,256]{1,0:T(1,128)} %param.22) | copy-start | bytes 3076
  138.5 3.2 collective-permute-start.7
  144.8 6.4 %collective-permute-start.8 = (bf16[2,2560]{1,0:T(2,128)(2,1)S(1)}, bf16[2,2560]{1,0:T(2,128)(2,1)S(1)}, u32[]{:S(2)}, u32[]{:S(2)}) collective-permute-start(bf16[2,2560]{1,0:T(2,128)(2,1)S(1)} %fusion.131), channel_id=1, source_target_pairs={{0,4},{4,8},{8,12},{12,16},{16,20},{20,24},{24,28},{28,0},{1,5},{5... | collective-permute-start | bytes 30728 | tf_op jit(solution)/shard_map/ppermute | solution.py:19
  151.2 6.4 %collective-permute-start.9 = (bf16[2,2560]{1,0:T(2,128)(2,1)S(1)}, bf16[2,2560]{1,0:T(2,128)(2,1)S(1)}, u32[]{:S(2)}, u32[]{:S(2)}) collective-permute-start(bf16[2,2560]{1,0:T(2,128)(2,1)S(1)} %collective-permute-done.8), channel_id=1, source_target_pairs={{0,4},{4,8},{8,12},{12,16},{16,20},{20,24},{24,28},{28,0},{1,5},{5... | collective-permute-start | bytes 30728 | tf_op jit(solution)/shard_map/ppermute | solution.py:19
  157.6 6.4 %collective-permute-start.10 = (bf16[2,2560]{1,0:T(2,128)(2,1)S(1)}, bf16[2,2560]{1,0:T(2,128)(2,1)S(1)}, u32[]{:S(2)}, u32[]{:S(2)}) collective-permute-start(bf16[2,2560]{1,0:T(2,128)(2,1)S(1)} %collective-permute-done.9), channel_id=1, source_target_pairs={{0,4},{4,8},{8,12},{12,16},{16,20},{20,24},{24,28},{28,0},{1,5},{5... | collective-permute-start | bytes 30728 | tf_op jit(solution)/shard_map/ppermute | solution.py:19
  164.0 6.4 %collective-permute-start.11 = (bf16[2,2560]{1,0:T(2,128)(2,1)S(1)}, bf16[2,2560]{1,0:T(2,128)(2,1)S(1)}, u32[]{:S(2)}, u32[]{:S(2)}) collective-permute-start(bf16[2,2560]{1,0:T(2,128)(2,1)S(1)} %collective-permute-done.10), channel_id=1, source_target_pairs={{0,4},{4,8},{8,12},{12,16},{16,20},{20,24},{24,28},{28,0},{1,5},{5... | collective-permute-start | bytes 30728 | tf_op jit(solution)/shard_map/ppermute | solution.py:19
  170.3 6.4 %collective-permute-start.12 = (bf16[2,2560]{1,0:T(2,128)(2,1)S(1)}, bf16[2,2560]{1,0:T(2,128)(2,1)S(1)}, u32[]{:S(2)}, u32[]{:S(2)}) collective-permute-start(bf16[2,2560]{1,0:T(2,128)(2,1)S(1)} %collective-permute-done.11), channel_id=1, source_target_pairs={{0,4},{4,8},{8,12},{12,16},{16,20},{20,24},{24,28},{28,0},{1,5},{5... | collective-permute-start | bytes 30728 | tf_op jit(solution)/shard_map/ppermute | solution.py:19
  170.9 171.2 %collective-permute-start.15 = (f32[2]{0:T(128)S(1)}, f32[2]{0:T(128)S(1)}, u32[]{:S(2)}, u32[]{:S(2)}) collective-permute-start(f32[2]{0:T(128)S(1)} %slice_convert_fusion), channel_id=1, source_target_pairs={{2,0},{3,1},{6,4},{7,5},{10,8},{11,9},{14,12},{15,13},{18,16},{19,... | collective-permute-start | bytes 32 | tf_op jit(solution)/shard_map/ppermute | solution.py:28
  176.7 6.4 %collective-permute-start.13 = (bf16[2,2560]{1,0:T(2,128)(2,1)S(1)}, bf16[2,2560]{1,0:T(2,128)(2,1)S(1)}, u32[]{:S(2)}, u32[]{:S(2)}) collective-permute-start(bf16[2,2560]{1,0:T(2,128)(2,1)S(1)} %collective-permute-done.12), channel_id=1, source_target_pairs={{0,4},{4,8},{8,12},{12,16},{16,20},{20,24},{24,28},{28,0},{1,5},{5... | collective-permute-start | bytes 30728 | tf_op jit(solution)/shard_map/ppermute | solution.py:19
  183.1 6.4 %collective-permute-start.14 = (bf16[2,2560]{1,0:T(2,128)(2,1)S(1)}, bf16[2,2560]{1,0:T(2,128)(2,1)S(1)}, u32[]{:S(2)}, u32[]{:S(2)}) collective-permute-start(bf16[2,2560]{1,0:T(2,128)(2,1)S(1)} %collective-permute-done.13), channel_id=1, source_target_pairs={{0,4},{4,8},{8,12},{12,16},{16,20},{20,24},{24,28},{28,0},{1,5},{5... | collective-permute-start | bytes 30728 | tf_op jit(solution)/shard_map/ppermute | solution.py:19
  189.8 93.3 %copy-start.4 = (pred[2]{0:T(512)(128)(4,1)S(1)}, pred[2]{0:T(512)(128)(4,1)}, u32[]{:S(2)}) copy-start(pred[2]{0:T(512)(128)(4,1)} %copy-done.3) | copy-start | bytes 10
  214.7 194.3 %all-reduce.17.cloned.1.call-start = ((), (), s32[]{:S(2)}) async-start(), calls=%async_computation.3 | async-start | bytes 163840
  342.1 115.3 %all-reduce.11.cloned.1.call-start = ((), (), s32[]{:S(2)}) async-start(), calls=%async_computation | async-start | bytes 327680 | tf_op jit(solution)/shard_map/psum | solution.py:213
  410.9 3.1 collective-permute-start.16
Sparse Core Ops, SparseCore 0:
  66.6 69.4 all-reduce.12
  214.8 68.2 all-reduce.14
  342.2 66.7 all-reduce.16
  438.1 19.1 all-reduce.10
